TPU v7x, 128 devices: a whole 4x4x4 slice. The times are simulated.
128 devices in a mesh: vel: 32 (over x_hi, y, z), space: 4 (over x_lo, core).
Axes of the slice: x: 4 (x_hi: 2, x_lo: 2; x = x_hi * 2 + x_lo), y: 4, z: 4, core: 2. Of those that a mesh axis runs over, the one named last changes fastest.
Arguments:
- dist: float32 [4096, 32, 1024], P('vel', 'space'), may hold values from -6 to 6
- vel_index: int32 [3, 4096], P(None, 'vel'), may hold values from 0 to 15, as said below
- relax: float32 [32, 1024], P('space'), may hold values from 0.05 to 0.9
- wall_mask: int32 [32, 1024], P('space'), may hold values 0 or 1
- macro_inverse: float32 [13, 13], replicated, may hold values from -1.5 to 1.5
Outputs:
- dist_out: float32 [4096, 32, 1024], P('vel', 'space')
- macro_fields: float32 [13, 32, 1024], P(None, 'space', 'vel')
- change_norm: float32 [2], replicated
Inputs may be any that keep to these rules, and one draw needn't show every extreme that they name: `vel_index`: each point of the velocity grid of 4096 points appears in exactly one column.
All inputs are finite; a program needn't handle non-finite values. No bound on the sum of `wall_mask` on one device may be relied on, other than what follows from the above.
Results may differ from a plain program's by a relative error of at most 0.0003.
Values sent between devices are 32-bit elements; how exact they have to be, the bound alone decides.
A program may use at most 128 MiB of HBM per device.

v0:
```python
import math
import jax
import jax.numpy as jnp
from jax import lax
from jax.sharding import PartitionSpec as P

NVX = 16
NY = 64
NZ = 16
MOM = 13
SWEEPS = 3
ITERS = 2
speed_range = 4.0
time_step = 0.08
coupling = 0.5


def with_halo(shard, sides, width):
    for axis, dim in sides:
        peers, length = (lax.axis_size(axis), shard.shape[dim])
        up = [(i, (i + 1) % peers) for i in range(peers)]
        down = [(j, i) for i, j in up]
        last = lax.slice_in_dim(shard, length - width, length, axis=dim)
        first = lax.slice_in_dim(shard, 0, width, axis=dim)
        before = lax.ppermute(last, axis, up)
        after = lax.ppermute(first, axis, down)
        shard = jnp.concatenate([before, shard, after], axis=dim)
    return shard


def velocities(vel_index):
    return speed_range * (2.0 * vel_index.astype(jnp.float32) + 1.0 - NVX) / NVX


def bases(velocity):
    cxv, cyv, czv = (velocity[0], velocity[1], velocity[2])
    square = cxv * cxv + cyv * cyv + czv * czv
    weights = (2.0 * speed_range / NVX) ** 3 * math.pi ** (-1.5) * jnp.exp(-square)
    heat = square - 2.5
    functions = jnp.stack(
        [
            jnp.ones_like(cxv),
            cxv,
            cyv,
            czv,
            2.0 * square / 3.0 - 1.0,
            2.0 * cxv * cyv,
            2.0 * cxv * czv,
            2.0 * cyv * czv,
            cxv * cxv - cyv * cyv,
            cyv * cyv - czv * czv,
            cxv * heat,
            cyv * heat,
            czv * heat,
        ],
        0,
    )
    moment_rows = functions * weights[None, :]
    factor = 4.0 / 15.0
    shakhov = jnp.stack(
        [
            jnp.ones_like(cxv),
            2.0 * cxv,
            2.0 * cyv,
            2.0 * czv,
            square - 1.5,
            factor * cxv * heat,
            factor * cyv * heat,
            factor * czv * heat,
        ],
        1,
    )
    walls = jnp.stack([jnp.ones_like(cxv), square - 1.5], 1)
    return (moment_rows, shakhov, walls)


def upwind_local(block, speed, axis):
    lower = jnp.roll(block, 1, axis)
    higher = jnp.roll(block, -1, axis)
    return jnp.where(speed > 0, block - lower, higher - block)


def stream(dist, velocity):
    count, width, cells = dist.shape
    padded = with_halo(dist, (("space", 1),), 1)
    lower_x = padded[:, :-2]
    higher_x = padded[:, 2:]
    cxv = velocity[0][:, None, None]
    cyv = velocity[1][:, None, None, None]
    czv = velocity[2][:, None, None, None]
    along_x = jnp.where(cxv > 0, dist - lower_x, higher_x - dist)
    grid = dist.reshape(count, width, NY, NZ)
    across = cyv * upwind_local(grid, cyv, 2) + czv * upwind_local(grid, czv, 3)
    total = cxv * along_x + across.reshape(count, width, cells)
    return dist - time_step * total


def slab_sweep(field):
    padded = with_halo(field, (("space", 1),), 1)
    beside_all = padded[:, :-2] + padded[:, 2:]
    for axis in (2, 3):
        beside_all = beside_all + jnp.roll(field, 1, axis) + jnp.roll(field, -1, axis)
    return beside_all


def smooth(local, neighbours):
    rows, width, cells = local.shape
    source = local[1:5].reshape(4, width, cells // NZ, NZ)
    field = source
    for sweep in range(SWEEPS):
        field = (source + coupling * neighbours(field)) / (1.0 + 6.0 * coupling)
    return jnp.concatenate([local[0:1], field.reshape(4, width, cells), local[5:]], 0)


def shards(dist, vel_index, relax, wall_mask, macro_inverse):
    highest = lax.Precision.HIGHEST
    count, width, cells = dist.shape
    share = cells // lax.axis_size("vel")
    velocity = velocities(vel_index)
    moment_rows, shakhov, walls = bases(velocity)
    norms = []
    owned_block = None
    for step in range(ITERS):
        read = stream(dist, velocity)
        partial_moments = jnp.dot(
            moment_rows, read.reshape(count, width * cells), precision=highest
        ).reshape(MOM, width, cells)
        totals = lax.psum(partial_moments, "vel")
        local = jnp.einsum("kj,jxc->kxc", macro_inverse, totals, precision=highest)
        updated = smooth(local, slab_sweep)
        change = lax.psum(jnp.sum((updated - totals) ** 2), "space")
        fields = jnp.concatenate([updated[0:5], updated[10:13]], 0)
        owned_block = lax.dynamic_slice_in_dim(updated, lax.axis_index("vel") * share, share, 2)
        norms.append(jnp.sqrt(change))
        flat_fields = fields.reshape(8, width * cells)
        target = jnp.dot(shakhov, flat_fields, precision=highest).reshape(count, width, cells)
        wall_fields = jnp.stack([flat_fields[0], flat_fields[4]], 0)
        wall_value = jnp.dot(walls, wall_fields, precision=highest).reshape(count, width, cells)
        dist = jnp.where(wall_mask[None] > 0, wall_value, read + relax[None] * (target - read))
    return (dist, owned_block, jnp.stack(norms))


def solution(mesh):
    return jax.shard_map(
        shards,
        mesh=mesh,
        in_specs=(P("vel", "space", None), P(None, "vel"), P("space", None), P("space", None), P()),
        out_specs=(P("vel", "space", None), P(None, "space", "vel"), P()),
        check_vma=False,
    )
```

profile of v0, /device:TPU:0, one launch (start us, length us, event | category | flops | bytes accessed | tf_op | source)
XLA Modules:
  0.0 973.2 jit_solution(570978027934620654)
XLA Ops:
  7.2 4.6 copy.217
  16.8 5.4 copy.208
  22.2 4.1 fusion.104
  28.3 4.1 pad_maximum_fusion.4
  32.3 4.2 pad_maximum_fusion.6
  36.6 5.3 copy.210
  41.9 5.4 copy.211
  47.3 5.4 copy.214
  52.7 5.3 copy.215
  58.2 13.7 %fusion.12 = f32[128,8,1024]{2,0,1:T(8,128)} fusion(f32[128,8,1024]{2,0,1:T(8,128)} %copy-done.4, f32[128,1,1024]{2,0,1:T(8,128)} %collective-permute-done.1, f32[128,1,1024]{2,0,1:T(8,128)S(1)} %collective-permute-done, f32[128,8,1024]{2,0,1:T(8,128)} %copy.215, f32[128,8,1024]{2,0,1:T(8,128)} %copy.214, f32[128,8,1024]{2,0,1:T(8,128)} %copy.211, ...), kind=kLoop, calls=%fused_computation.16 | loop fusion | flops 18874368 | bytes 26216320 | tf_op jit(solution)/shard_map/sub | solution.py:95
  71.9 5.3 copy.218
  77.2 6.5 fusion.16
  84.1 355.4 %all-reduce.5.cloned.1.call-done = f32[13,8,1024]{2,0,1:T(8,128)} async-done(((f32[13,8,1024]{2,0,1:T(8,128)}), f32[13,8,1024]{2,0,1:T(8,128)}) %all-reduce.5.cloned.1.call-update) | async-done | bytes 426000 | tf_op jit(solution)/shard_map/psum | solution.py:128
  466.6 5.7 bitcast_select_fusion
  472.3 5.3 copy.221
  477.6 4.1 fusion.99
  482.2 4.1 fusion.101
  495.9 5.3 copy.222
  501.2 5.4 copy.223
  506.6 4.8 pad_maximum_fusion.10
  511.4 5.4 copy.224
  516.8 4.7 pad_maximum_fusion.11
  521.5 5.4 copy.225
  526.9 13.5 %fusion.5 = f32[128,8,1024]{2,0,1:T(8,128)} fusion(f32[128,8,1024]{2,0,1:T(8,128)} %bitcast_select_fusion, f32[128,1,1024]{2,0,1:T(8,128)S(1)} %collective-permute-done.9, f32[128,1,1024]{2,0,1:T(8,128)S(1)} %collective-permute-done.8, f32[128,8,1024]{2,0,1:T(8,128)} %copy.225, f32[128,8,1024]{2,0,1:T(8,128)} %copy.224, f32[128,8,1024]{2,0,1:T(8,128)} %copy.223, ...), kind=kLoop, calls=%fused_computation.7 | loop fusion | flops 18874368 | bytes 26216320 | tf_op jit(solution)/shard_map/sub | solution.py:95
  540.4 5.3 copy.226
  545.7 6.5 fusion.14
  553.8 351.6 %all-reduce.7.cloned.1.call-done = f32[13,8,1024]{2,0,1:T(8,128)} async-done(((f32[13,8,1024]{2,0,1:T(8,128)}), f32[13,8,1024]{2,0,1:T(8,128)}) %all-reduce.7.cloned.1.call-update) | async-done | bytes 426000 | tf_op jit(solution)/shard_map/psum | solution.py:128
  929.8 8.1 all-reduce.1
  940.2 8.2 fusion.72
  948.4 5.3 copy.229
  953.8 7.2 add_select_fusion
  961.0 4.4 copy.232
  (142 shorter events, 71.4 us)
Async XLA Ops:
  7.2 432.4 %copy-start = (f32[13,13]{1,0:T(8,128)S(1)}, f32[13,13]{1,0:T(8,128)}, u32[]{:S(2)}) copy-start(f32[13,13]{1,0:T(8,128)} %param.9) | copy-start | bytes 2032
  7.2 432.3 %all-reduce.5.cloned.1.call-start = ((), (), s32[]{:S(2)}) async-start(), calls=%async_computation | async-start | bytes 1048576 | tf_op jit(solution)/shard_map/psum | solution.py:128
  11.8 2.0 copy-start.4
  14.9 43.2 %collective-permute-start = (f32[128,1,1024]{2,0,1:T(8,128)}, f32[128,1,1024]{2,0,1:T(8,128)S(1)}, u32[]{:S(2)}, u32[]{:S(2)}) collective-permute-start(f32[128,1,1024]{2,0,1:T(8,128)} %get-tuple-element.37), channel_id=1, source_target_pairs={{0,1},{1,2},{2,3},{3,0},{4,5},{5,6},{6,7},{7,4},{8,9},{9,10},{10,1... | collective-permute-start | bytes 1572872 | tf_op jit(solution)/shard_map/ppermute | solution.py:25
  14.9 43.3 %collective-permute-start.1 = (f32[128,1,1024]{2,0,1:T(8,128)}, f32[128,1,1024]{2,0,1:T(8,128)}, u32[]{:S(2)}, u32[]{:S(2)}) collective-permute-start(f32[128,1,1024]{2,0,1:T(8,128)} %get-tuple-element.38), channel_id=1, source_target_pairs={{1,0},{2,1},{3,2},{0,3},{5,4},{6,5},{7,6},{4,7},{9,8},{10,9},{11,1... | collective-permute-start | bytes 1572872 | tf_op jit(solution)/shard_map/ppermute | solution.py:26
  22.2 4.6 copy-start.1
  26.9 1.4 copy-start.9
  77.2 6.8 copy-start.8
  83.7 821.7 %all-reduce.7.cloned.1.call-start = ((), (), s32[]{:S(2)}) async-start(), calls=%async_computation.1 | async-start | bytes 1048576 | tf_op jit(solution)/shard_map/psum | solution.py:128
  442.6 5.0 collective-permute-start.2
  442.7 4.9 collective-permute-start.3
  449.6 4.9 collective-permute-start.4
  450.4 4.2 collective-permute-start.5
  456.6 4.5 collective-permute-start.6
  457.4 3.9 collective-permute-start.7
  462.3 4.4 copy-start.7
  463.0 3.6 copy-start.3
  477.6 4.6 copy-start.2
  489.1 37.8 %collective-permute-start.8 = (f32[128,1,1024]{2,0,1:T(8,128)}, f32[128,1,1024]{2,0,1:T(8,128)S(1)}, u32[]{:S(2)}, u32[]{:S(2)}) collective-permute-start(f32[128,1,1024]{2,0,1:T(8,128)} %get-tuple-element.27), channel_id=1, source_target_pairs={{0,1},{1,2},{2,3},{3,0},{4,5},{5,6},{6,7},{7,4},{8,9},{9,10},{10,1... | collective-permute-start | bytes 1572872 | tf_op jit(solution)/shard_map/ppermute | solution.py:25
  490.1 36.8 %collective-permute-start.9 = (f32[128,1,1024]{2,0,1:T(8,128)}, f32[128,1,1024]{2,0,1:T(8,128)S(1)}, u32[]{:S(2)}, u32[]{:S(2)}) collective-permute-start(f32[128,1,1024]{2,0,1:T(8,128)} %get-tuple-element.28), channel_id=1, source_target_pairs={{1,0},{2,1},{3,2},{0,3},{5,4},{6,5},{7,6},{4,7},{9,8},{10,9},{11,1... | collective-permute-start | bytes 1572872 | tf_op jit(solution)/shard_map/ppermute | solution.py:26
  545.7 7.3 copy-start.5
  908.6 4.8 collective-permute-start.10
  908.6 4.7 collective-permute-start.11
  915.3 4.7 collective-permute-start.12
  916.3 3.8 collective-permute-start.13
  922.1 4.6 collective-permute-start.14
  923.1 3.6 collective-permute-start.15
  926.7 2.3 copy-start.6
Sparse Core Ops, SparseCore 0:
  83.9 355.6 all-reduce.4
  552.4 352.9 all-reduce.6
where the time goes:
time: 977 us; the launch traced here: 973 us
  waiting for transfers between devices  724 us (74%)
  local copies, waits for them, and re-layouts  110 us (11%)
  other arithmetic  57.9 us (6%)
  matrix products  40.9 us (4%)
  between operations  16.3 us (2%)
  starting transfers between devices  15.7 us (2%)
    psum x2, waiting for transfers between devices, shards(): totals = lax.psum(partial_moments, 'vel')  707 us
    sub x2, other arithmetic, stream(): return dist - time_step * total  27.2 us
    concatenate x4, local copies, waits for them, and re-layouts, upwind_local(): higher = jnp.roll(block, -1, axis)  21.6 us
    concatenate x4, local copies, waits for them, and re-layouts, upwind_local(): lower = jnp.roll(block, 1, axis)  21.4 us
  transfers between devices with their start and end apart: 18, of which 9 were waited for; matrix products, arithmetic and copies ran while one was open for 8% of the time, Pallas kernels for 0%

commit v1 on v0

--- a/solution.py
+++ b/solution.py
@@ -125,7 +125,13 @@
         partial_moments = jnp.dot(
             moment_rows, read.reshape(count, width * cells), precision=highest
         ).reshape(MOM, width, cells)
-        totals = lax.psum(partial_moments, "vel")
+
+        def step_on_meshes(view):
+            e_next = lax.all_gather(view, axis_name="vel")
+            back = jnp.sum(e_next, axis=0)
+            return back
+
+        totals = step_on_meshes(partial_moments)
         local = jnp.einsum("kj,jxc->kxc", macro_inverse, totals, precision=highest)
         updated = smooth(local, slab_sweep)
         change = lax.psum(jnp.sum((updated - totals) ** 2), "space")

time: 977 us -> 556 us (0.57)
  waiting for transfers between devices: 724 us -> 291 us
  other arithmetic: 57.9 us -> 70.8 us
    psum x2 -> x0, waiting for transfers between devices: 707 us -> none  [shards(): totals = lax.psum(partial_moments, 'vel')]
    all_gather x0 -> x2, waiting for transfers between devices: none -> 273 us  [step_on_meshes(): e_next = lax.all_gather(view, axis_name='vel')]
    reduce_sum x0 -> x2, other arithmetic: none -> 12.4 us  [step_on_meshes(): back = jnp.sum(e_next, axis=0)]
  transfers between devices with their start and end apart: 18 -> 18, of which waited for: 9 -> 8; matrix products, arithmetic and copies ran while one was open for 8% -> 14% of each run, Pallas kernels for 0% -> 0%
where the time goes in v1:
time: 556 us; the launch traced here: 552 us
  waiting for transfers between devices  291 us (52%)
  local copies, waits for them, and re-layouts  113 us (20%)
  other arithmetic  70.8 us (13%)
  matrix products  37.8 us (7%)
  between operations  16.2 us (3%)
  starting transfers between devices  15.4 us (3%)
  blocking collectives  7.79 us (1%)
    all_gather x2, waiting for transfers between devices, step_on_meshes(): e_next = lax.all_gather(view, axis_name='vel')  273 us
    sub x2, other arithmetic, stream(): return dist - time_step * total  27.4 us
    concatenate x4, local copies, waits for them, and re-layouts, upwind_local(): higher = jnp.roll(block, -1, axis)  21.6 us
    concatenate x4, local copies, waits for them, and re-layouts, upwind_local(): lower = jnp.roll(block, 1, axis)  21.5 us
    unnamed x20, local copies, waits for them, and re-layouts  18.1 us
    ppermute x8, waiting for transfers between devices, with_halo(): before = lax.ppermute(last, axis, up)  17.4 us
    concatenate x4, other arithmetic, upwind_local(): lower = jnp.roll(block, 1, axis)  15.5 us
    slice x8, local copies, waits for them, and re-layouts, upwind_local(): lower = jnp.roll(block, 1, axis)  14.2 us
  transfers between devices with their start and end apart: 18, of which 8 were waited for; matrix products, arithmetic and copies ran while one was open for 14% of the time, Pallas kernels for 0%

profile of v1, /device:TPU:0, one launch (start us, length us, event | category | flops | bytes accessed | tf_op | source)
XLA Modules:
  0.0 551.6 jit_solution(12788485454242428569)
XLA Ops:
  7.2 4.6 copy.225
  17.1 5.4 copy.216
  22.5 4.1 fusion.108
  32.7 4.2 pad_maximum_fusion.6
  36.9 5.4 copy.218
  42.3 5.4 copy.219
  47.7 5.4 copy.222
  53.1 5.3 copy.223
  58.6 13.7 %fusion.12 = f32[128,8,1024]{2,0,1:T(8,128)} fusion(f32[128,8,1024]{2,0,1:T(8,128)} %copy-done.4, f32[128,1,1024]{2,0,1:T(8,128)} %collective-permute-done.1, f32[128,1,1024]{2,0,1:T(8,128)S(1)} %collective-permute-done, f32[128,8,1024]{2,0,1:T(8,128)} %copy.223, f32[128,8,1024]{2,0,1:T(8,128)} %copy.222, f32[128,8,1024]{2,0,1:T(8,128)} %copy.219, ...), kind=kLoop, calls=%fused_computation.16 | loop fusion | flops 18874368 | bytes 26216320 | tf_op jit(solution)/shard_map/sub | solution.py:95
  72.3 5.3 copy.226
  77.6 5.7 %fusion.16 = f32[13,8,1024]{2,0,1:T(8,128)S(1)} fusion(f32[128,8,1024]{0,2,1:T(8,128)} %copy.226, f32[13,128]{1,0:T(8,128)S(1)} %stack.18, f32[128]{0:T(128)S(1)} %get-tuple-element.120), kind=kOutput, calls=%fused_computation.29 | convolution fusion | flops 163579520 | bytes 4627456 | tf_op jit(solution)/shard_map/dot_general | solution.py:125
  84.6 138.8 %all-gather.5.cloned.1.call-done = f32[416,8,1024]{2,1,0:T(8,128)} async-done(((f32[13,8,1024]{2,1,0:T(8,128)}), f32[416,8,1024]{2,1,0:T(8,128)}) %all-gather.5.cloned.1.call-update) | async-done | bytes 13631504 | tf_op jit(solution)/shard_map/all_gather | solution.py:130
  223.4 6.2 %reduce_sum.36 = f32[13,8,1024]{2,1,0:T(8,128)S(1)} reduce(f32[32,13,8,1024]{3,2,1,0:T(8,128)} %bitcast.119, f32[]{:T(128)} %constant.52.clone.1), dimensions={0}, to_apply=%region_0.1 | reduce | flops 3301376 | bytes 14057476 | tf_op jit(solution)/shard_map/reduce_sum | solution.py:131
  255.8 5.7 %bitcast_select_fusion = f32[128,8,1024]{2,0,1:T(8,128)} fusion(f32[16,8,8,1024]{3,2,1,0:T(8,128)S(1)} %bitcast.109, f32[128,8,1024]{2,0,1:T(8,128)S(1)} %copy-done.3, f32[8,1024,8]{1,2,0:T(8,128)S(1)} %bitcast.121, f32[8,1024]{1,0:T(8,128)S(1)} %copy-done.5, pred[8,1024]{1,0:T(8,128)(4,1)S(1)} %broadcast_compare_fusion, f32[128,8]{0,1:T(8,128)S(1)} %stack.20), kind=kOutput, calls=%fused_computation | convolution fusion | flops 104857600 | bytes 12890112 | tf_op jit(solution)/shard_map/dot_general | solution.py:142
  261.5 5.3 copy.231
  266.9 4.1 fusion.103
  284.8 5.3 copy.232
  290.2 5.4 copy.233
  295.6 4.8 pad_maximum_fusion.10
  300.4 5.4 copy.234
  305.8 4.7 pad_maximum_fusion.11
  310.5 5.3 copy.235
  315.9 13.7 %fusion.5 = f32[128,8,1024]{2,0,1:T(8,128)} fusion(f32[128,8,1024]{2,0,1:T(8,128)} %bitcast_select_fusion, f32[128,1,1024]{2,0,1:T(8,128)} %collective-permute-done.9, f32[128,1,1024]{2,0,1:T(8,128)S(1)} %collective-permute-done.8, f32[128,8,1024]{2,0,1:T(8,128)} %copy.235, f32[128,8,1024]{2,0,1:T(8,128)} %copy.234, f32[128,8,1024]{2,0,1:T(8,128)} %copy.233, ...), kind=kLoop, calls=%fused_computation.7 | loop fusion | flops 18874368 | bytes 26216320 | tf_op jit(solution)/shard_map/sub | solution.py:95
  329.6 5.8 %copy.236 = f32[128,8,1024]{0,2,1:T(8,128)} copy(f32[128,8,1024]{2,0,1:T(8,128)} %fusion.5) | data formatting | bytes 8388608 | tf_op jit(solution)/shard_map/sub | solution.py:95
  335.4 5.7 %fusion.14 = f32[13,8,1024]{2,0,1:T(8,128)S(1)} fusion(f32[128,8,1024]{0,2,1:T(8,128)} %copy.236, f32[13,128]{1,0:T(8,128)S(1)} %stack.18, f32[128]{0:T(128)S(1)} %get-tuple-element.120), kind=kOutput, calls=%fused_computation.27 | convolution fusion | flops 163579520 | bytes 4627456 | tf_op jit(solution)/shard_map/dot_general | solution.py:125
  343.8 134.5 %all-gather.7.cloned.1.call-done = f32[416,8,1024]{2,1,0:T(8,128)} async-done(((f32[13,8,1024]{2,1,0:T(8,128)}), f32[416,8,1024]{2,1,0:T(8,128)}) %all-gather.7.cloned.1.call-update) | async-done | bytes 13631504 | tf_op jit(solution)/shard_map/all_gather | solution.py:130
  478.3 6.2 %reduce_sum.37 = f32[13,8,1024]{2,1,0:T(8,128)S(1)} reduce(f32[32,13,8,1024]{3,2,1,0:T(8,128)} %bitcast.118, f32[]{:T(128)} %constant.52.clone.1), dimensions={0}, to_apply=%region_1.2 | reduce | flops 3301376 | bytes 14057476 | tf_op jit(solution)/shard_map/reduce_sum | solution.py:131
  508.5 7.8 %all-reduce.1 = (f32[]{:T(128)}, f32[]{:T(128)}) all-reduce(f32[]{:T(128)} %get-tuple-element.99, f32[]{:T(128)} %fusion.69), channel_id=1, replica_groups=mesh['vel'=32,'space'=4] {'space'}, use_global_device_ids=true, to_apply=%region_5.6 | all-reduce | flops 2 | bytes 16 | tf_op jit(solution)/shard_map/psum | solution.py:137
  518.6 8.2 %fusion.76 = f32[128,8192]{0,1:T(8,128)} fusion(f32[1,8192]{1,0:T(1,128)S(1)} %slice.499, f32[1,8192]{1,0:T(1,128)S(1)} %bitcast.124, f32[128,1]{0,1:T(1,128)S(1)} %get-tuple-element.122), kind=kOutput, calls=%fused_computation.109 | convolution fusion | flops 25182208 | bytes 4260352 | tf_op jit(solution)/shard_map/dot_general | solution.py:144
  526.8 5.3 copy.241
  532.2 7.3 %add_select_fusion = f32[128,8,1024]{2,0,1:T(8,128)S(1)} fusion(f32[128,8,1024]{2,0,1:T(8,128)} %copy.241, f32[128,8,1024]{2,0,1:T(8,128)} %fusion.5, f32[8,1024,8]{1,2,0:T(8,128)S(1)} %bitcast.120, f32[8,1024]{1,0:T(8,128)S(1)} %copy-done.5, pred[8,1024]{1,0:T(8,128)(4,1)S(1)} %broadcast_compare_fusion, f32[128,8]{0,1:T(8,128)S(1)} %stack.20), kind=kOutput, calls=%fused_computation.31 | convolution fusion | flops 104857600 | bytes 12890112 | tf_op jit(solution)/shard_map/dot_general | solution.py:142
  539.5 4.4 copy.246
  (142 shorter events, 80.6 us)
Async XLA Ops:
  7.2 222.4 %copy-start = (f32[13,13]{1,0:T(8,128)S(1)}, f32[13,13]{1,0:T(8,128)}, u32[]{:S(2)}) copy-start(f32[13,13]{1,0:T(8,128)} %param.9) | copy-start | bytes 2032
  7.2 216.2 %all-gather.5.cloned.1.call-start = ((), (), s32[]{:S(2)}) async-start(), calls=%async_computation | async-start | bytes 14057472 | tf_op jit(solution)/shard_map/all_gather | solution.py:130
  11.8 2.0 copy-start.4
  14.9 43.6 %collective-permute-start = (f32[128,1,1024]{2,0,1:T(8,128)}, f32[128,1,1024]{2,0,1:T(8,128)S(1)}, u32[]{:S(2)}, u32[]{:S(2)}) collective-permute-start(f32[128,1,1024]{2,0,1:T(8,128)} %get-tuple-element.37), channel_id=1, source_target_pairs={{0,1},{1,2},{2,3},{3,0},{4,5},{5,6},{6,7},{7,4},{8,9},{9,10},{10,1... | collective-permute-start | bytes 1572872 | tf_op jit(solution)/shard_map/ppermute | solution.py:25
  14.9 43.7 %collective-permute-start.1 = (f32[128,1,1024]{2,0,1:T(8,128)}, f32[128,1,1024]{2,0,1:T(8,128)}, u32[]{:S(2)}, u32[]{:S(2)}) collective-permute-start(f32[128,1,1024]{2,0,1:T(8,128)} %get-tuple-element.38), channel_id=1, source_target_pairs={{1,0},{2,1},{3,2},{0,3},{5,4},{6,5},{7,6},{4,7},{9,8},{10,9},{11,1... | collective-permute-start | bytes 1572872 | tf_op jit(solution)/shard_map/ppermute | solution.py:26
  22.5 4.6 copy-start.1
  27.2 1.4 copy-start.7
  77.6 7.0 %copy-start.6 = (s32[8,1024]{1,0:T(8,128)S(1)}, s32[8,1024]{1,0:T(8,128)}, u32[]{:S(2)}) copy-start(s32[8,1024]{1,0:T(8,128)} %param.8) | copy-start | bytes 98308
  84.3 394.0 %all-gather.7.cloned.1.call-start = ((), (), s32[]{:S(2)}) async-start(), calls=%async_computation.1 | async-start | bytes 14057472 | tf_op jit(solution)/shard_map/all_gather | solution.py:130
  232.0 5.0 collective-permute-start.2
  232.1 4.9 collective-permute-start.3
  238.9 4.9 collective-permute-start.4
  239.7 4.2 collective-permute-start.5
  245.9 4.6 collective-permute-start.6
  246.7 3.8 collective-permute-start.7
  251.5 4.4 copy-start.5
  252.2 3.6 copy-start.3
  266.9 4.6 copy-start.2
  278.3 37.6 %collective-permute-start.8 = (f32[128,1,1024]{2,0,1:T(8,128)}, f32[128,1,1024]{2,0,1:T(8,128)S(1)}, u32[]{:S(2)}, u32[]{:S(2)}) collective-permute-start(f32[128,1,1024]{2,0,1:T(8,128)} %get-tuple-element.27), channel_id=1, source_target_pairs={{0,1},{1,2},{2,3},{3,0},{4,5},{5,6},{6,7},{7,4},{8,9},{9,10},{10,1... | collective-permute-start | bytes 1572872 | tf_op jit(solution)/shard_map/ppermute | solution.py:25
  279.4 36.5 %collective-permute-start.9 = (f32[128,1,1024]{2,0,1:T(8,128)}, f32[128,1,1024]{2,0,1:T(8,128)}, u32[]{:S(2)}, u32[]{:S(2)}) collective-permute-start(f32[128,1,1024]{2,0,1:T(8,128)} %get-tuple-element.28), channel_id=1, source_target_pairs={{1,0},{2,1},{3,2},{0,3},{5,4},{6,5},{7,6},{4,7},{9,8},{10,9},{11,1... | collective-permute-start | bytes 1572872 | tf_op jit(solution)/shard_map/ppermute | solution.py:26
  486.9 5.0 collective-permute-start.10
  486.9 4.9 collective-permute-start.11
  493.8 4.8 collective-permute-start.12
  494.6 4.0 collective-permute-start.13
  500.6 4.7 collective-permute-start.14
  501.6 3.7 collective-permute-start.15
Sparse Core Ops, SparseCore 0:
  84.4 138.9 all-gather.4
  342.2 136.0 all-gather.6
